TPU v7x, 512 devices: a whole 4x4x16 slice. The times are simulated.
512 devices in a mesh: ad: 64 (over z, x), tp: 8 (over y, core).
Axes of the slice: x: 4, y: 4, z: 16, core: 2. Of those that a mesh axis runs over, the one named last changes fastest.
Arguments:
- tokens: bfloat16 [4, 3072, 8192], P(None, 'ad', 'tp'), may hold values from -6 to 6
- row_adapter_index: int32 [4, 3072], P(None, 'ad'), may hold values from 0 to 255, as said below
- key_base_weight: bfloat16 [8192, 1024], P('tp'), may hold values from -0.0625 to 0.0625
- adapter_down_weight: bfloat16 [256, 8192, 64], P('ad', 'tp'), may hold values from -0.0625 to 0.0625
- adapter_up_weight: bfloat16 [256, 64, 1024], P('ad', None, 'tp'), may hold values from -0.75 to 0.75
Outputs:
- token_keys_output: bfloat16 [4, 3072, 1024], P(None, 'ad', 'tp')
Inputs may be any that keep to these rules, and one draw needn't show every extreme that they name: `row_adapter_index`: group g holds adapters g * 4 to (g + 1) * 4 - 1. In each step the 48 rows of one index of ad name one group in exactly 2 rows and every other group in at most 1 row; that busiest group is the same for every index of ad in a step, so it receives 2 rows from each.
All inputs are finite; a program needn't handle non-finite values.
Results may differ from a plain program's by a relative error of at most 0.005.
Values may be sent and summed in bfloat16 or wider, within the bound.
A program may use at most 64 MiB of HBM per device.

v0:
```python
import jax
import jax.numpy as jnp
from jax import lax
from jax.sharding import PartitionSpec as P


def adapter_row_output(outgoing_rows, row_labels, down_weight_tile, up_weight_tile):
    adapter_number = down_weight_tile.shape[0]
    row_count = outgoing_rows.shape[0]
    down_all = jnp.einsum(
        "nd,adr->nar", outgoing_rows, down_weight_tile, preferred_element_type=jnp.float32
    )
    labels = (jnp.arange(adapter_number, dtype=jnp.int32) + 1).astype(jnp.bfloat16)
    selector = (row_labels[:, None] == labels[None, :]).astype(jnp.float32)
    down_part = jnp.sum(down_all * selector[:, :, None], axis=1)
    down_sum = lax.psum(down_part, "tp")
    down_low = down_sum.astype(jnp.bfloat16)
    spread_rows = (selector.astype(jnp.bfloat16)[:, :, None] * down_low[:, None, :]).reshape(
        row_count, -1
    )
    up_flat = up_weight_tile.reshape(
        adapter_number * up_weight_tile.shape[1], up_weight_tile.shape[2]
    )
    return jnp.dot(spread_rows, up_flat, preferred_element_type=jnp.float32).astype(jnp.bfloat16)


def body(tokens, row_adapter_index, key_base_weight, adapter_down_weight, adapter_up_weight):
    step_count, row_dev, width_per_shard = tokens.shape
    groups = lax.axis_size("ad")
    adapter_number = adapter_down_weight.shape[0]
    capacity = max(2, 3 * row_dev // groups)
    gathered_rows = tokens.reshape(step_count * row_dev, width_per_shard)
    partial_base = jnp.dot(gathered_rows, key_base_weight, preferred_element_type=jnp.float32)
    base_keys_output = lax.psum_scatter(partial_base, "tp", scatter_dimension=1, tiled=True)
    key_feature_width = base_keys_output.shape[1]
    outputs = []
    for step_index in range(step_count):
        step_rows = tokens[step_index]
        row_index_list = row_adapter_index[step_index]
        owner_group = row_index_list // adapter_number
        local_index = row_index_list % adapter_number
        group_hits = (owner_group[:, None] == jnp.arange(groups, dtype=jnp.int32)[None, :]).astype(
            jnp.int32
        )
        slot_rank = jnp.sum((jnp.cumsum(group_hits, axis=0) - group_hits) * group_hits, axis=1)
        tag_values = (local_index + 1).astype(jnp.float32)
        stays_remote = owner_group >= 0
        slot_index = jnp.where(stays_remote, owner_group * capacity + slot_rank, -1)
        dispatch = (
            slot_index[None, :] == jnp.arange(groups * capacity, dtype=jnp.int32)[:, None]
        ).astype(jnp.bfloat16)
        send_rows = jnp.dot(dispatch, step_rows, preferred_element_type=jnp.float32).astype(
            jnp.bfloat16
        )
        send_rows = send_rows.reshape(groups, capacity, width_per_shard)
        send_tags = (
            jnp.dot(dispatch.astype(jnp.float32), tag_values)
            .astype(jnp.bfloat16)
            .reshape(groups, capacity)
        )
        incoming_rows = lax.all_to_all(send_rows, "ad", split_axis=0, concat_axis=0, tiled=True)
        incoming_labels = lax.all_to_all(send_tags, "ad", split_axis=0, concat_axis=0, tiled=True)
        sender_number, slot_number = incoming_labels.shape
        adapter_update = adapter_row_output(
            incoming_rows.reshape(-1, width_per_shard),
            incoming_labels.reshape(-1),
            adapter_down_weight,
            adapter_up_weight,
        )
        adapter_update = adapter_update.reshape(sender_number, slot_number, key_feature_width)
        rows_sent_back = lax.all_to_all(
            adapter_update, "ad", split_axis=0, concat_axis=0, tiled=True
        )
        routed = jnp.dot(
            dispatch.T,
            rows_sent_back.reshape(groups * capacity, key_feature_width),
            preferred_element_type=jnp.float32,
        )
        step_base = base_keys_output[step_index * row_dev : (step_index + 1) * row_dev]
        outputs.append(step_base + routed)
    return jnp.stack(outputs).astype(jnp.bfloat16)


def solution(mesh):
    placed = (
        P(None, "ad", "tp"),
        P(None, "ad"),
        P("tp", None),
        P("ad", "tp", None),
        P("ad", None, "tp"),
    )
    return jax.shard_map(
        body, mesh=mesh, in_specs=placed, out_specs=P(None, "ad", "tp"), check_vma=False
    )
```

profile of v0, /device:TPU:2, one launch (start us, length us, event | category | flops | bytes accessed | tf_op | source)
XLA Modules:
  0.0 308.1 jit_solution(69769566374800532)
XLA Ops:
  6.5 0.9 and_select_fusion.10
  8.0 0.2 select_reduce_fusion.2
  8.2 0.2 select_reduce_fusion
  8.4 0.9 fusion.56
  9.4 0.8 all_to_all.67
  10.3 18.6 %all-to-all-start.9 = ((bf16[64,1,2]{2,1,0:T(2,128)(2,1)}), bf16[64,1,2]{2,1,0:T(2,128)(2,1)S(1)}, u32[]{:S(2)}, u32[]{:S(2)}) async-start(bf16[64,1,2]{2,1,0:T(2,128)(2,1)} %all_to_all.67), calls=%async_computation.10 | async-start | bytes 65536 | tf_op jit(solution)/shard_map/all_to_all | solution.py:62
  29.0 0.8 all_to_all.65
  29.9 12.9 %all-to-all-done.9 = bf16[64,1,2]{2,1,0:T(2,128)(2,1)S(1)} async-done(((bf16[64,1,2]{2,1,0:T(2,128)(2,1)}), bf16[64,1,2]{2,1,0:T(2,128)(2,1)S(1)}, u32[]{:S(2)}, u32[]{:S(2)}) %all-to-all-start.9) | async-done | bytes 288 | tf_op jit(solution)/shard_map/all_to_all | solution.py:62
  42.7 5.5 %all-to-all-start.3 = ((bf16[64,1,2]{2,1,0:T(2,128)(2,1)}), bf16[64,1,2]{2,1,0:T(2,128)(2,1)S(1)}, u32[]{:S(2)}, u32[]{:S(2)}) async-start(bf16[64,1,2]{2,1,0:T(2,128)(2,1)} %all_to_all.65), calls=%async_computation.4 | async-start | bytes 65536 | tf_op jit(solution)/shard_map/all_to_all | solution.py:62
  48.3 0.8 all_to_all.66
  49.1 12.7 %all-to-all-done.3 = bf16[64,1,2]{2,1,0:T(2,128)(2,1)S(1)} async-done(((bf16[64,1,2]{2,1,0:T(2,128)(2,1)}), bf16[64,1,2]{2,1,0:T(2,128)(2,1)S(1)}, u32[]{:S(2)}, u32[]{:S(2)}) %all-to-all-start.3) | async-done | bytes 288 | tf_op jit(solution)/shard_map/all_to_all | solution.py:62
  61.8 5.6 %all-to-all-start.6 = ((bf16[64,1,2]{2,1,0:T(2,128)(2,1)}), bf16[64,1,2]{2,1,0:T(2,128)(2,1)S(1)}, u32[]{:S(2)}, u32[]{:S(2)}) async-start(bf16[64,1,2]{2,1,0:T(2,128)(2,1)} %all_to_all.66), calls=%async_computation.7 | async-start | bytes 65536 | tf_op jit(solution)/shard_map/all_to_all | solution.py:62
  67.6 0.8 all_to_all.64
  68.4 12.9 %all-to-all-done.6 = bf16[64,1,2]{2,1,0:T(2,128)(2,1)S(1)} async-done(((bf16[64,1,2]{2,1,0:T(2,128)(2,1)}), bf16[64,1,2]{2,1,0:T(2,128)(2,1)S(1)}, u32[]{:S(2)}, u32[]{:S(2)}) %all-to-all-start.6) | async-done | bytes 288 | tf_op jit(solution)/shard_map/all_to_all | solution.py:62
  81.4 0.6 copy-done.5
  82.0 5.5 %all-to-all-start = ((bf16[64,1,2]{2,1,0:T(2,128)(2,1)}), bf16[64,1,2]{2,1,0:T(2,128)(2,1)S(1)}, u32[]{:S(2)}, u32[]{:S(2)}) async-start(bf16[64,1,2]{2,1,0:T(2,128)(2,1)} %all_to_all.64), calls=%async_computation.1 | async-start | bytes 65536 | tf_op jit(solution)/shard_map/all_to_all | solution.py:62
  87.5 1.1 convolution_convert_fusion.3
  88.6 0.8 reshape.453
  89.4 11.9 %all-to-all-done = bf16[64,1,2]{2,1,0:T(2,128)(2,1)S(1)} async-done(((bf16[64,1,2]{2,1,0:T(2,128)(2,1)}), bf16[64,1,2]{2,1,0:T(2,128)(2,1)S(1)}, u32[]{:S(2)}, u32[]{:S(2)}) %all-to-all-start) | async-done | bytes 288 | tf_op jit(solution)/shard_map/all_to_all | solution.py:62
  101.3 5.5 %all-to-all-start.1 = ((bf16[64,2,1024]{2,1,0:T(2,128)(2,1)}), bf16[64,2,1024]{2,1,0:T(2,128)(2,1)S(1)}, u32[]{:S(2)}, u32[]{:S(2)}) async-start(bf16[64,2,1024]{2,1,0:T(2,128)(2,1)} %reshape.453), calls=%async_computation.2 | async-start | bytes 524288 | tf_op jit(solution)/shard_map/all_to_all | solution.py:61
  106.8 0.2 convolution_convert_fusion.1
  107.0 0.8 reshape.461
  107.8 16.6 %all-to-all-done.1 = bf16[64,2,1024]{2,1,0:T(2,128)(2,1)S(1)} async-done(((bf16[64,2,1024]{2,1,0:T(2,128)(2,1)}), bf16[64,2,1024]{2,1,0:T(2,128)(2,1)S(1)}, u32[]{:S(2)}, u32[]{:S(2)}) %all-to-all-start.1) | async-done | bytes 262176 | tf_op jit(solution)/shard_map/all_to_all | solution.py:61
  124.5 5.7 %all-to-all-start.7 = ((bf16[64,2,1024]{2,1,0:T(2,128)(2,1)}), bf16[64,2,1024]{2,1,0:T(2,128)(2,1)S(1)}, u32[]{:S(2)}, u32[]{:S(2)}) async-start(bf16[64,2,1024]{2,1,0:T(2,128)(2,1)} %reshape.461), calls=%async_computation.8 | async-start | bytes 524288 | tf_op jit(solution)/shard_map/all_to_all | solution.py:61
  130.2 0.2 convolution_convert_fusion.2
  130.4 0.8 reshape.457
  131.2 16.9 %all-to-all-done.7 = bf16[64,2,1024]{2,1,0:T(2,128)(2,1)S(1)} async-done(((bf16[64,2,1024]{2,1,0:T(2,128)(2,1)}), bf16[64,2,1024]{2,1,0:T(2,128)(2,1)S(1)}, u32[]{:S(2)}, u32[]{:S(2)}) %all-to-all-start.7) | async-done | bytes 262176 | tf_op jit(solution)/shard_map/all_to_all | solution.py:61
  148.1 6.3 %all-to-all-start.4 = ((bf16[64,2,1024]{2,1,0:T(2,128)(2,1)}), bf16[64,2,1024]{2,1,0:T(2,128)(2,1)}, u32[]{:S(2)}, u32[]{:S(2)}) async-start(bf16[64,2,1024]{2,1,0:T(2,128)(2,1)} %reshape.457), calls=%async_computation.5 | async-start | bytes 524288 | tf_op jit(solution)/shard_map/all_to_all | solution.py:61
  154.4 1.5 fusion.100
  156.0 0.9 convolution_convert_fusion
  156.9 1.8 reshape.465
  158.6 0.9 reduce.3
  159.5 0.1 eq.243
  159.6 0.9 reduce.1
  160.7 0.9 reduce.2
  161.7 0.9 reduce
  162.7 0.7 fusion.52
  163.5 8.6 %all-to-all-done.4 = bf16[64,2,1024]{2,1,0:T(2,128)(2,1)} async-done(((bf16[64,2,1024]{2,1,0:T(2,128)(2,1)}), bf16[64,2,1024]{2,1,0:T(2,128)(2,1)}, u32[]{:S(2)}, u32[]{:S(2)}) %all-to-all-start.4) | async-done | bytes 262176 | tf_op jit(solution)/shard_map/all_to_all | solution.py:61
  172.1 6.6 %all-to-all-start.10 = ((bf16[64,2,1024]{2,1,0:T(2,128)(2,1)}), bf16[64,2,1024]{2,1,0:T(2,128)(2,1)S(1)}, u32[]{:S(2)}, u32[]{:S(2)}) async-start(bf16[64,2,1024]{2,1,0:T(2,128)(2,1)} %reshape.465), calls=%async_computation.11 | async-start | bytes 524288 | tf_op jit(solution)/shard_map/all_to_all | solution.py:61
  178.7 0.3 fusion.101
  179.0 0.6 multiply_reduce_fusion.3
  179.8 0.3 fusion.103
  180.2 1.1 reshape.458
  181.2 0.3 fusion.102
  181.6 15.0 %all-to-all-done.10 = bf16[64,2,1024]{2,1,0:T(2,128)(2,1)S(1)} async-done(((bf16[64,2,1024]{2,1,0:T(2,128)(2,1)}), bf16[64,2,1024]{2,1,0:T(2,128)(2,1)S(1)}, u32[]{:S(2)}, u32[]{:S(2)}) %all-to-all-start.10) | async-done | bytes 262176 | tf_op jit(solution)/shard_map/all_to_all | solution.py:61
  196.6 0.3 fusion.104
  197.0 25.0 %all-reduce.2 = (bf16[128,64]{0,1:T(8,128)(2,1)S(1)}, bf16[128,64]{0,1:T(8,128)(2,1)S(1)}, bf16[128,64]{0,1:T(8,128)(2,1)S(1)}, bf16[128,64]{0,1:T(8,128)(2,1)S(1)}) all-reduce(f32[128,64]{0,1:T(8,128)S(1)} %multiply_reduce_fusion, f32[128,64]{0,1:T(8,128)S(1)} %multiply_reduce_fusion.1, ...), channel_id=1, replica_groups=mesh['ad'=64,'tp'=8] {'tp'}, use_global_device_ids=true, to_apply=%region_16.17 | all-reduce | flops 32768 | bytes 196608 | tf_op jit(solution)/shard_map/psum | solution.py:16
  222.0 0.8 fusion.3
  222.8 5.5 %all-to-all-start.11 = ((bf16[64,2,128]{2,1,0:T(2,128)(2,1)}), bf16[64,2,128]{2,1,0:T(2,128)(2,1)S(1)}, u32[]{:S(2)}, u32[]{:S(2)}) async-start(bf16[64,2,128]{2,1,0:T(2,128)(2,1)} %bitcast.50), calls=%async_computation.12 | async-start | bytes 65536 | tf_op jit(solution)/shard_map/all_to_all | solution.py:71
  228.3 0.8 fusion.2
  229.1 12.9 %all-to-all-done.11 = bf16[64,2,128]{2,1,0:T(2,128)(2,1)S(1)} async-done(((bf16[64,2,128]{2,1,0:T(2,128)(2,1)}), bf16[64,2,128]{2,1,0:T(2,128)(2,1)S(1)}, u32[]{:S(2)}, u32[]{:S(2)}) %all-to-all-start.11) | async-done | bytes 32800 | tf_op jit(solution)/shard_map/all_to_all | solution.py:71
  242.0 5.2 %all-to-all-start.8 = ((bf16[64,2,128]{2,1,0:T(2,128)(2,1)}), bf16[64,2,128]{2,1,0:T(2,128)(2,1)S(1)}, u32[]{:S(2)}, u32[]{:S(2)}) async-start(bf16[64,2,128]{2,1,0:T(2,128)(2,1)} %bitcast.37), calls=%async_computation.9 | async-start | bytes 65536 | tf_op jit(solution)/shard_map/all_to_all | solution.py:71
  247.2 0.8 fusion.1
  248.1 13.1 %all-to-all-done.8 = bf16[64,2,128]{2,1,0:T(2,128)(2,1)S(1)} async-done(((bf16[64,2,128]{2,1,0:T(2,128)(2,1)}), bf16[64,2,128]{2,1,0:T(2,128)(2,1)S(1)}, u32[]{:S(2)}, u32[]{:S(2)}) %all-to-all-start.8) | async-done | bytes 32800 | tf_op jit(solution)/shard_map/all_to_all | solution.py:71
  261.1 5.5 %all-to-all-start.5 = ((bf16[64,2,128]{2,1,0:T(2,128)(2,1)}), bf16[64,2,128]{2,1,0:T(2,128)(2,1)S(1)}, u32[]{:S(2)}, u32[]{:S(2)}) async-start(bf16[64,2,128]{2,1,0:T(2,128)(2,1)} %bitcast.24), calls=%async_computation.6 | async-start | bytes 65536 | tf_op jit(solution)/shard_map/all_to_all | solution.py:71
  266.6 0.8 fusion
  267.4 0.9 fusion.8
  268.3 11.9 %all-to-all-done.5 = bf16[64,2,128]{2,1,0:T(2,128)(2,1)S(1)} async-done(((bf16[64,2,128]{2,1,0:T(2,128)(2,1)}), bf16[64,2,128]{2,1,0:T(2,128)(2,1)S(1)}, u32[]{:S(2)}, u32[]{:S(2)}) %all-to-all-start.5) | async-done | bytes 32800 | tf_op jit(solution)/shard_map/all_to_all | solution.py:71
  280.2 5.5 %all-to-all-start.2 = ((bf16[64,2,128]{2,1,0:T(2,128)(2,1)}), bf16[64,2,128]{2,1,0:T(2,128)(2,1)S(1)}, u32[]{:S(2)}, u32[]{:S(2)}) async-start(bf16[64,2,128]{2,1,0:T(2,128)(2,1)} %bitcast.11), calls=%async_computation.3 | async-start | bytes 65536 | tf_op jit(solution)/shard_map/all_to_all | solution.py:71
  285.8 0.9 fusion.9
  286.7 0.9 fusion.10
  287.7 12.0 %all-to-all-done.2 = bf16[64,2,128]{2,1,0:T(2,128)(2,1)S(1)} async-done(((bf16[64,2,128]{2,1,0:T(2,128)(2,1)}), bf16[64,2,128]{2,1,0:T(2,128)(2,1)S(1)}, u32[]{:S(2)}, u32[]{:S(2)}) %all-to-all-start.2) | async-done | bytes 32800 | tf_op jit(solution)/shard_map/all_to_all | solution.py:71
  299.7 0.9 fusion.11
  300.6 0.6 pad_maximum_fusion
  (66 shorter events, 2.1 us)
Async XLA Ops:
  6.5 147.9 %copy-start = (bf16[1024,1024]{1,0:T(8,128)(2,1)S(1)}, bf16[1024,1024]{1,0:T(8,128)(2,1)}, u32[]{:S(2)}) copy-start(bf16[1024,1024]{1,0:T(8,128)(2,1)} %param.7) | copy-start | bytes 6291460
  6.5 100.3 %copy-start.2 = (bf16[4,48,1024]{2,1,0:T(8,128)(2,1)S(1)}, bf16[4,48,1024]{2,1,0:T(8,128)(2,1)}, u32[]{:S(2)}) copy-start(bf16[4,48,1024]{2,1,0:T(8,128)(2,1)} %param.5) | copy-start | bytes 1179652
  9.3 121.9 %copy-start.8 = (s32[48]{0:T(128)}, s32[48]{0:T(128)S(1)}, u32[]{:S(2)}) copy-start(s32[48]{0:T(128)S(1)} %get-tuple-element.17) | copy-start | bytes 580
  9.3 121.9 %copy-start.10 = (s32[48]{0:T(128)}, s32[48]{0:T(128)S(1)}, u32[]{:S(2)}) copy-start(s32[48]{0:T(128)S(1)} %get-tuple-element.19) | copy-start | bytes 580
  9.3 121.9 %copy-start.12 = (s32[48]{0:T(128)}, s32[48]{0:T(128)S(1)}, u32[]{:S(2)}) copy-start(s32[48]{0:T(128)S(1)} %get-tuple-element.18) | copy-start | bytes 580
  9.3 146.6 %copy-start.14 = (s32[48]{0:T(128)}, s32[48]{0:T(128)S(1)}, u32[]{:S(2)}) copy-start(s32[48]{0:T(128)S(1)} %get-tuple-element.20) | copy-start | bytes 580
  10.3 32.5 %all-to-all-start.9 = ((bf16[64,1,2]{2,1,0:T(2,128)(2,1)}), bf16[64,1,2]{2,1,0:T(2,128)(2,1)S(1)}, u32[]{:S(2)}, u32[]{:S(2)}) async-start(bf16[64,1,2]{2,1,0:T(2,128)(2,1)} %all_to_all.67), calls=%async_computation.10 | async-start | bytes 65536 | tf_op jit(solution)/shard_map/all_to_all | solution.py:62
  42.7 38.6 %copy-start.3 = (bf16[64,1,2]{2,1,0:T(2,128)(2,1)}, bf16[64,1,2]{2,1,0:T(2,128)(2,1)S(1)}, u32[]{:S(2)}) copy-start(bf16[64,1,2]{2,1,0:T(2,128)(2,1)S(1)} %all-to-all-done.9) | copy-start | bytes 772
  42.7 19.1 %all-to-all-start.3 = ((bf16[64,1,2]{2,1,0:T(2,128)(2,1)}), bf16[64,1,2]{2,1,0:T(2,128)(2,1)S(1)}, u32[]{:S(2)}, u32[]{:S(2)}) async-start(bf16[64,1,2]{2,1,0:T(2,128)(2,1)} %all_to_all.65), calls=%async_computation.4 | async-start | bytes 65536 | tf_op jit(solution)/shard_map/all_to_all | solution.py:62
  61.8 19.5 %copy-start.4 = (bf16[64,1,2]{2,1,0:T(2,128)(2,1)}, bf16[64,1,2]{2,1,0:T(2,128)(2,1)S(1)}, u32[]{:S(2)}) copy-start(bf16[64,1,2]{2,1,0:T(2,128)(2,1)S(1)} %all-to-all-done.3) | copy-start | bytes 772
  61.8 19.5 %all-to-all-start.6 = ((bf16[64,1,2]{2,1,0:T(2,128)(2,1)}), bf16[64,1,2]{2,1,0:T(2,128)(2,1)S(1)}, u32[]{:S(2)}, u32[]{:S(2)}) async-start(bf16[64,1,2]{2,1,0:T(2,128)(2,1)} %all_to_all.66), calls=%async_computation.7 | async-start | bytes 65536 | tf_op jit(solution)/shard_map/all_to_all | solution.py:62
  81.4 0.6 copy-start.5
  82.0 19.3 %all-to-all-start = ((bf16[64,1,2]{2,1,0:T(2,128)(2,1)}), bf16[64,1,2]{2,1,0:T(2,128)(2,1)S(1)}, u32[]{:S(2)}, u32[]{:S(2)}) async-start(bf16[64,1,2]{2,1,0:T(2,128)(2,1)} %all_to_all.64), calls=%async_computation.1 | async-start | bytes 65536 | tf_op jit(solution)/shard_map/all_to_all | solution.py:62
  101.3 53.2 %copy-start.6 = (bf16[64,1,2]{2,1,0:T(2,128)(2,1)}, bf16[64,1,2]{2,1,0:T(2,128)(2,1)S(1)}, u32[]{:S(2)}) copy-start(bf16[64,1,2]{2,1,0:T(2,128)(2,1)S(1)} %all-to-all-done) | copy-start | bytes 772
  101.3 23.2 %all-to-all-start.1 = ((bf16[64,2,1024]{2,1,0:T(2,128)(2,1)}), bf16[64,2,1024]{2,1,0:T(2,128)(2,1)S(1)}, u32[]{:S(2)}, u32[]{:S(2)}) async-start(bf16[64,2,1024]{2,1,0:T(2,128)(2,1)} %reshape.453), calls=%async_computation.2 | async-start | bytes 524288 | tf_op jit(solution)/shard_map/all_to_all | solution.py:61
  124.5 23.7 %all-to-all-start.7 = ((bf16[64,2,1024]{2,1,0:T(2,128)(2,1)}), bf16[64,2,1024]{2,1,0:T(2,128)(2,1)S(1)}, u32[]{:S(2)}, u32[]{:S(2)}) async-start(bf16[64,2,1024]{2,1,0:T(2,128)(2,1)} %reshape.461), calls=%async_computation.8 | async-start | bytes 524288 | tf_op jit(solution)/shard_map/all_to_all | solution.py:61
  148.1 24.0 %all-to-all-start.4 = ((bf16[64,2,1024]{2,1,0:T(2,128)(2,1)}), bf16[64,2,1024]{2,1,0:T(2,128)(2,1)}, u32[]{:S(2)}, u32[]{:S(2)}) async-start(bf16[64,2,1024]{2,1,0:T(2,128)(2,1)} %reshape.457), calls=%async_computation.5 | async-start | bytes 524288 | tf_op jit(solution)/shard_map/all_to_all | solution.py:61
  154.4 113.0 %reduce-scatter.2.cloned.1.call-start = ((), (), s32[]{:S(2)}) async-start(), calls=%async_computation.13 | async-start | bytes 884736 | tf_op jit(solution)/shard_map/reduce_scatter | solution.py:34
  155.9 22.8 %copy-start.1 = (bf16[4,1024,64]{1,2,0:T(8,128)(2,1)S(1)}, bf16[4,1024,64]{1,2,0:T(8,128)(2,1)}, u32[]{:S(2)}) copy-start(bf16[4,1024,64]{1,2,0:T(8,128)(2,1)} %param.8) | copy-start | bytes 1572868
  172.1 24.4 %all-to-all-start.10 = ((bf16[64,2,1024]{2,1,0:T(2,128)(2,1)}), bf16[64,2,1024]{2,1,0:T(2,128)(2,1)S(1)}, u32[]{:S(2)}, u32[]{:S(2)}) async-start(bf16[64,2,1024]{2,1,0:T(2,128)(2,1)} %reshape.465), calls=%async_computation.11 | async-start | bytes 524288 | tf_op jit(solution)/shard_map/all_to_all | solution.py:61
  179.7 17.2 %copy-start.7 = (f32[128,64]{0,1:T(8,128)S(1)}, f32[128,64]{0,1:T(8,128)}, u32[]{:S(2)}) copy-start(f32[128,64]{0,1:T(8,128)} %multiply_reduce_fusion.3) | copy-start | bytes 98308
  179.7 42.2 %copy-start.19 = (bf16[128,4]{0,1:T(4,128)(2,1)S(1)}, bf16[128,4]{0,1:T(4,128)(2,1)}, u32[]{:S(2)}) copy-start(bf16[128,4]{0,1:T(4,128)(2,1)} %get-tuple-element.40) | copy-start | bytes 3076
  179.8 42.2 %copy-start.20 = (bf16[4,64,128]{2,1,0:T(8,128)(2,1)S(1)}, bf16[4,64,128]{2,1,0:T(8,128)(2,1)}, u32[]{:S(2)}) copy-start(bf16[4,64,128]{2,1,0:T(8,128)(2,1)} %param.9) | copy-start | bytes 196612
  180.1 48.2 %copy-start.18 = (bf16[128,4]{0,1:T(4,128)(2,1)S(1)}, bf16[128,4]{0,1:T(4,128)(2,1)}, u32[]{:S(2)}) copy-start(bf16[128,4]{0,1:T(4,128)(2,1)} %get-tuple-element.38) | copy-start | bytes 3076
  180.1 67.1 %copy-start.17 = (bf16[128,4]{0,1:T(4,128)(2,1)S(1)}, bf16[128,4]{0,1:T(4,128)(2,1)}, u32[]{:S(2)}) copy-start(bf16[128,4]{0,1:T(4,128)(2,1)} %get-tuple-element.36) | copy-start | bytes 3076
  180.1 86.5 %copy-start.16 = (bf16[128,4]{0,1:T(4,128)(2,1)S(1)}, bf16[128,4]{0,1:T(4,128)(2,1)}, u32[]{:S(2)}) copy-start(bf16[128,4]{0,1:T(4,128)(2,1)} %get-tuple-element.27) | copy-start | bytes 3076
  180.1 87.3 %copy-start.15 = (s32[48]{0:T(128)S(1)}, s32[48]{0:T(128)}, u32[]{:S(2)}) copy-start(s32[48]{0:T(128)} %copy-done.14) | copy-start | bytes 580
  180.1 105.6 %copy-start.13 = (s32[48]{0:T(128)S(1)}, s32[48]{0:T(128)}, u32[]{:S(2)}) copy-start(s32[48]{0:T(128)} %copy-done.12) | copy-start | bytes 580
  180.2 106.6 %copy-start.11 = (s32[48]{0:T(128)S(1)}, s32[48]{0:T(128)}, u32[]{:S(2)}) copy-start(s32[48]{0:T(128)} %copy-done.10) | copy-start | bytes 580
  180.2 119.5 %copy-start.9 = (s32[48]{0:T(128)S(1)}, s32[48]{0:T(128)}, u32[]{:S(2)}) copy-start(s32[48]{0:T(128)} %copy-done.8) | copy-start | bytes 580
  222.8 19.2 %all-to-all-start.11 = ((bf16[64,2,128]{2,1,0:T(2,128)(2,1)}), bf16[64,2,128]{2,1,0:T(2,128)(2,1)S(1)}, u32[]{:S(2)}, u32[]{:S(2)}) async-start(bf16[64,2,128]{2,1,0:T(2,128)(2,1)} %bitcast.50), calls=%async_computation.12 | async-start | bytes 65536 | tf_op jit(solution)/shard_map/all_to_all | solution.py:71
  242.0 19.1 %all-to-all-start.8 = ((bf16[64,2,128]{2,1,0:T(2,128)(2,1)}), bf16[64,2,128]{2,1,0:T(2,128)(2,1)S(1)}, u32[]{:S(2)}, u32[]{:S(2)}) async-start(bf16[64,2,128]{2,1,0:T(2,128)(2,1)} %bitcast.37), calls=%async_computation.9 | async-start | bytes 65536 | tf_op jit(solution)/shard_map/all_to_all | solution.py:71
  261.1 19.1 %all-to-all-start.5 = ((bf16[64,2,128]{2,1,0:T(2,128)(2,1)}), bf16[64,2,128]{2,1,0:T(2,128)(2,1)S(1)}, u32[]{:S(2)}, u32[]{:S(2)}) async-start(bf16[64,2,128]{2,1,0:T(2,128)(2,1)} %bitcast.24), calls=%async_computation.6 | async-start | bytes 65536 | tf_op jit(solution)/shard_map/all_to_all | solution.py:71
  280.2 19.4 %all-to-all-start.2 = ((bf16[64,2,128]{2,1,0:T(2,128)(2,1)}), bf16[64,2,128]{2,1,0:T(2,128)(2,1)S(1)}, u32[]{:S(2)}, u32[]{:S(2)}) async-start(bf16[64,2,128]{2,1,0:T(2,128)(2,1)} %bitcast.11), calls=%async_computation.3 | async-start | bytes 65536 | tf_op jit(solution)/shard_map/all_to_all | solution.py:71
Sparse Core Ops, SparseCore 0:
  158.0 40.8 reduce-scatter.1
where the time goes:
time: 309 us; the launch traced here: 308 us
  waiting for transfers between devices  157 us (51%)
  starting transfers between devices  81 us (26%)
  blocking collectives  25 us (8%)
  between operations  13.9 us (4%)
  matrix products  12.6 us (4%)
  local copies, waits for them, and re-layouts  10 us (3%)
  other arithmetic  8.13 us (3%)
    all_to_all x4, waiting for transfers between devices, body(): lax.all_to_all(send_rows, 'ad', split_axis=0, concat_axis=0, tiled=True)  57.2 us
    all_to_all x4, waiting for transfers between devices, body(): lax.all_to_all(send_tags, 'ad', split_axis=0, concat_axis=0, tiled=True)  50.4 us
    all_to_all x4, waiting for transfers between devices, body(): lax.all_to_all(adapter_update, 'ad', split_axis=0, concat_axis=0, tiled=T...  49.9 us
    all_to_all x4, starting transfers between devices, body(): lax.all_to_all(send_tags, 'ad', split_axis=0, concat_axis=0, tiled=True)  35.2 us
    psum x1, blocking collectives, adapter_row_output(): down_sum = lax.psum(down_part, 'tp')  25 us
    all_to_all x4, starting transfers between devices, body(): lax.all_to_all(send_rows, 'ad', split_axis=0, concat_axis=0, tiled=True)  24.1 us
    all_to_all x4, starting transfers between devices, body(): lax.all_to_all(adapter_update, 'ad', split_axis=0, concat_axis=0, tiled=T...  21.6 us
  transfers between devices with their start and end apart: 13, of which 12 were waited for; matrix products, arithmetic and copies ran while one was open for 7% of the time, Pallas kernels for 0%

commit v1 on v0

--- a/solution.py
+++ b/solution.py
@@ -13,7 +13,9 @@
     labels = (jnp.arange(adapter_number, dtype=jnp.int32) + 1).astype(jnp.bfloat16)
     selector = (row_labels[:, None] == labels[None, :]).astype(jnp.float32)
     down_part = jnp.sum(down_all * selector[:, :, None], axis=1)
-    down_sum = lax.psum(down_part, "tp")
+    down_sum = down_part
+    for hop in (1, 2, 4):
+        down_sum = down_sum + lax.ppermute(down_sum, "tp", [(dev, dev ^ hop) for dev in range(8)])
     down_low = down_sum.astype(jnp.bfloat16)
     spread_rows = (selector.astype(jnp.bfloat16)[:, :, None] * down_low[:, None, :]).reshape(
         row_count, -1

time: 309 us -> 320 us (1.036)
  the two profiles are of different devices: /device:TPU:2 before, /device:TPU:16 now
where the time goes in v1:
time: 320 us; the launch traced here: 318 us
  waiting for transfers between devices  164 us (51%)
  starting transfers between devices  107 us (33%)
  between operations  14.2 us (4%)
  matrix products  11.9 us (4%)
  local copies, waits for them, and re-layouts  11.7 us (4%)
  other arithmetic  9.01 us (3%)
    all_to_all x4, waiting for transfers between devices, body(): lax.all_to_all(send_rows, 'ad', split_axis=0, concat_axis=0, tiled=True)  56.6 us
    all_to_all x4, waiting for transfers between devices, body(): lax.all_to_all(send_tags, 'ad', split_axis=0, concat_axis=0, tiled=True)  54 us
    all_to_all x4, waiting for transfers between devices, body(): lax.all_to_all(adapter_update, 'ad', split_axis=0, concat_axis=0, tiled=T...  53.3 us
    ppermute x12, starting transfers between devices, adapter_row_output(): lax.ppermute(down_sum, 'tp', [(dev, dev ^ hop) for dev in range(8)])  34.7 us
    all_to_all x4, starting transfers between devices, body(): lax.all_to_all(send_tags, 'ad', split_axis=0, concat_axis=0, tiled=True)  32.2 us
    all_to_all x4, starting transfers between devices, body(): lax.all_to_all(send_rows, 'ad', split_axis=0, concat_axis=0, tiled=True)  20.2 us
    all_to_all x4, starting transfers between devices, body(): lax.all_to_all(adapter_update, 'ad', split_axis=0, concat_axis=0, tiled=T...  19.9 us
  transfers between devices with their start and end apart: 25, of which 12 were waited for; matrix products, arithmetic and copies ran while one was open for 7% of the time, Pallas kernels for 0%

profile of v1, /device:TPU:16, one launch (start us, length us, event | category | flops | bytes accessed | tf_op | source)
XLA Modules:
  0.0 317.7 jit_solution(8404462014916152015)
XLA Ops:
  6.5 0.9 and_select_fusion.10
  8.4 0.9 fusion.56
  9.4 0.8 all_to_all.64
  10.3 18.6 %all-to-all-start = ((bf16[64,1,2]{2,1,0:T(2,128)(2,1)}), bf16[64,1,2]{2,1,0:T(2,128)(2,1)S(1)}, u32[]{:S(2)}, u32[]{:S(2)}) async-start(bf16[64,1,2]{2,1,0:T(2,128)(2,1)} %all_to_all.64), calls=%async_computation.1 | async-start | bytes 65536 | tf_op jit(solution)/shard_map/all_to_all | solution.py:64
  29.0 0.8 all_to_all.65
  29.8 13.6 %all-to-all-done = bf16[64,1,2]{2,1,0:T(2,128)(2,1)S(1)} async-done(((bf16[64,1,2]{2,1,0:T(2,128)(2,1)}), bf16[64,1,2]{2,1,0:T(2,128)(2,1)S(1)}, u32[]{:S(2)}, u32[]{:S(2)}) %all-to-all-start) | async-done | bytes 288 | tf_op jit(solution)/shard_map/all_to_all | solution.py:64
  43.4 4.6 %all-to-all-start.3 = ((bf16[64,1,2]{2,1,0:T(2,128)(2,1)}), bf16[64,1,2]{2,1,0:T(2,128)(2,1)S(1)}, u32[]{:S(2)}, u32[]{:S(2)}) async-start(bf16[64,1,2]{2,1,0:T(2,128)(2,1)} %all_to_all.65), calls=%async_computation.4 | async-start | bytes 65536 | tf_op jit(solution)/shard_map/all_to_all | solution.py:64
  48.1 0.8 all_to_all.66
  48.9 13.9 %all-to-all-done.3 = bf16[64,1,2]{2,1,0:T(2,128)(2,1)S(1)} async-done(((bf16[64,1,2]{2,1,0:T(2,128)(2,1)}), bf16[64,1,2]{2,1,0:T(2,128)(2,1)S(1)}, u32[]{:S(2)}, u32[]{:S(2)}) %all-to-all-start.3) | async-done | bytes 288 | tf_op jit(solution)/shard_map/all_to_all | solution.py:64
  62.8 4.6 %all-to-all-start.6 = ((bf16[64,1,2]{2,1,0:T(2,128)(2,1)}), bf16[64,1,2]{2,1,0:T(2,128)(2,1)S(1)}, u32[]{:S(2)}, u32[]{:S(2)}) async-start(bf16[64,1,2]{2,1,0:T(2,128)(2,1)} %all_to_all.66), calls=%async_computation.7 | async-start | bytes 65536 | tf_op jit(solution)/shard_map/all_to_all | solution.py:64
  67.5 0.8 all_to_all.67
  68.3 13.6 %all-to-all-done.6 = bf16[64,1,2]{2,1,0:T(2,128)(2,1)S(1)} async-done(((bf16[64,1,2]{2,1,0:T(2,128)(2,1)}), bf16[64,1,2]{2,1,0:T(2,128)(2,1)S(1)}, u32[]{:S(2)}, u32[]{:S(2)}) %all-to-all-start.6) | async-done | bytes 288 | tf_op jit(solution)/shard_map/all_to_all | solution.py:64
  82.5 4.6 %all-to-all-start.9 = ((bf16[64,1,2]{2,1,0:T(2,128)(2,1)}), bf16[64,1,2]{2,1,0:T(2,128)(2,1)S(1)}, u32[]{:S(2)}, u32[]{:S(2)}) async-start(bf16[64,1,2]{2,1,0:T(2,128)(2,1)} %all_to_all.67), calls=%async_computation.10 | async-start | bytes 65536 | tf_op jit(solution)/shard_map/all_to_all | solution.py:64
  87.1 1.1 convolution_convert_fusion.3
  88.2 0.8 reshape.453
  89.0 12.9 %all-to-all-done.9 = bf16[64,1,2]{2,1,0:T(2,128)(2,1)S(1)} async-done(((bf16[64,1,2]{2,1,0:T(2,128)(2,1)}), bf16[64,1,2]{2,1,0:T(2,128)(2,1)S(1)}, u32[]{:S(2)}, u32[]{:S(2)}) %all-to-all-start.9) | async-done | bytes 288 | tf_op jit(solution)/shard_map/all_to_all | solution.py:64
  101.8 4.6 %all-to-all-start.1 = ((bf16[64,2,1024]{2,1,0:T(2,128)(2,1)}), bf16[64,2,1024]{2,1,0:T(2,128)(2,1)S(1)}, u32[]{:S(2)}, u32[]{:S(2)}) async-start(bf16[64,2,1024]{2,1,0:T(2,128)(2,1)} %reshape.453), calls=%async_computation.2 | async-start | bytes 524288 | tf_op jit(solution)/shard_map/all_to_all | solution.py:63
  106.7 0.8 reshape.457
  107.5 17.7 %all-to-all-done.1 = bf16[64,2,1024]{2,1,0:T(2,128)(2,1)S(1)} async-done(((bf16[64,2,1024]{2,1,0:T(2,128)(2,1)}), bf16[64,2,1024]{2,1,0:T(2,128)(2,1)S(1)}, u32[]{:S(2)}, u32[]{:S(2)}) %all-to-all-start.1) | async-done | bytes 262176 | tf_op jit(solution)/shard_map/all_to_all | solution.py:63
  125.9 4.6 %all-to-all-start.4 = ((bf16[64,2,1024]{2,1,0:T(2,128)(2,1)}), bf16[64,2,1024]{2,1,0:T(2,128)(2,1)S(1)}, u32[]{:S(2)}, u32[]{:S(2)}) async-start(bf16[64,2,1024]{2,1,0:T(2,128)(2,1)} %reshape.457), calls=%async_computation.5 | async-start | bytes 524288 | tf_op jit(solution)/shard_map/all_to_all | solution.py:63
  130.7 0.8 reshape.461
  131.5 17.7 %all-to-all-done.4 = bf16[64,2,1024]{2,1,0:T(2,128)(2,1)S(1)} async-done(((bf16[64,2,1024]{2,1,0:T(2,128)(2,1)}), bf16[64,2,1024]{2,1,0:T(2,128)(2,1)S(1)}, u32[]{:S(2)}, u32[]{:S(2)}) %all-to-all-start.4) | async-done | bytes 262176 | tf_op jit(solution)/shard_map/all_to_all | solution.py:63
  149.3 5.5 %all-to-all-start.7 = ((bf16[64,2,1024]{2,1,0:T(2,128)(2,1)}), bf16[64,2,1024]{2,1,0:T(2,128)(2,1)}, u32[]{:S(2)}, u32[]{:S(2)}) async-start(bf16[64,2,1024]{2,1,0:T(2,128)(2,1)} %reshape.461), calls=%async_computation.8 | async-start | bytes 524288 | tf_op jit(solution)/shard_map/all_to_all | solution.py:63
  155.0 0.8 reshape.465
  155.8 0.9 reduce
  156.8 0.9 reduce.1
  157.8 0.9 reduce.2
  158.8 0.9 reduce.3
  160.5 1.0 reshape.454
  161.5 11.8 %all-to-all-done.7 = bf16[64,2,1024]{2,1,0:T(2,128)(2,1)} async-done(((bf16[64,2,1024]{2,1,0:T(2,128)(2,1)}), bf16[64,2,1024]{2,1,0:T(2,128)(2,1)}, u32[]{:S(2)}, u32[]{:S(2)}) %all-to-all-start.7) | async-done | bytes 262176 | tf_op jit(solution)/shard_map/all_to_all | solution.py:63
  173.4 5.5 %all-to-all-start.10 = ((bf16[64,2,1024]{2,1,0:T(2,128)(2,1)}), bf16[64,2,1024]{2,1,0:T(2,128)(2,1)}, u32[]{:S(2)}, u32[]{:S(2)}) async-start(bf16[64,2,1024]{2,1,0:T(2,128)(2,1)} %reshape.465), calls=%async_computation.11 | async-start | bytes 524288 | tf_op jit(solution)/shard_map/all_to_all | solution.py:63
  179.8 1.9 collective-permute-start
  182.2 2.4 collective-permute-start.3
  184.6 1.0 reshape.462
  186.0 2.1 collective-permute-start.6
  188.1 9.4 %all-to-all-done.10 = bf16[64,2,1024]{2,1,0:T(2,128)(2,1)} async-done(((bf16[64,2,1024]{2,1,0:T(2,128)(2,1)}), bf16[64,2,1024]{2,1,0:T(2,128)(2,1)}, u32[]{:S(2)}, u32[]{:S(2)}) %all-to-all-start.10) | async-done | bytes 262176 | tf_op jit(solution)/shard_map/all_to_all | solution.py:63
  197.5 1.0 reshape.466
  198.9 1.9 collective-permute-start.9
  200.8 0.8 add.140
  201.6 3.2 %collective-permute-start.1 = (f32[128,64]{0,1:T(8,128)S(1)}, f32[128,64]{0,1:T(8,128)S(1)}, u32[]{:S(2)}, u32[]{:S(2)}) collective-permute-start(f32[128,64]{0,1:T(8,128)S(1)} %add.140), channel_id=1, source_target_pairs={{0,2},{1,3},{2,0},{3,1},{4,6},{5,7},{6,4},{7,5},{8,10},{9,11},{10,... | collective-permute-start | bytes 98312 | tf_op jit(solution)/shard_map/ppermute | solution.py:18
  204.8 2.7 collective-permute-start.4
  207.5 3.2 %collective-permute-start.7 = (f32[128,64]{0,1:T(8,128)S(1)}, f32[128,64]{0,1:T(8,128)S(1)}, u32[]{:S(2)}, u32[]{:S(2)}) collective-permute-start(f32[128,64]{0,1:T(8,128)S(1)} %add.154), channel_id=1, source_target_pairs={{0,2},{1,3},{2,0},{3,1},{4,6},{5,7},{6,4},{7,5},{8,10},{9,11},{10,... | collective-permute-start | bytes 98312 | tf_op jit(solution)/shard_map/ppermute | solution.py:18
  210.7 2.7 collective-permute-start.10
  213.4 2.2 collective-permute-start.2
  215.7 1.5 fusion.100
  217.3 5.1 %collective-permute-start.5 = (f32[128,64]{0,1:T(8,128)S(1)}, f32[128,64]{0,1:T(8,128)S(1)}, u32[]{:S(2)}, u32[]{:S(2)}) collective-permute-start(f32[128,64]{0,1:T(8,128)S(1)} %add.148), channel_id=1, source_target_pairs={{0,4},{1,5},{2,6},{3,7},{4,0},{5,1},{6,2},{7,3},{8,12},{9,13},{10,... | collective-permute-start | bytes 98312 | tf_op jit(solution)/shard_map/ppermute | solution.py:18
  222.4 2.2 collective-permute-start.8
  224.7 5.1 %collective-permute-start.11 = (f32[128,64]{0,1:T(8,128)S(1)}, f32[128,64]{0,1:T(8,128)S(1)}, u32[]{:S(2)}, u32[]{:S(2)}) collective-permute-start(f32[128,64]{0,1:T(8,128)S(1)} %add.162), channel_id=1, source_target_pairs={{0,4},{1,5},{2,6},{3,7},{4,0},{5,1},{6,2},{7,3},{8,12},{9,13},{10,... | collective-permute-start | bytes 98312 | tf_op jit(solution)/shard_map/ppermute | solution.py:18
  229.9 0.8 fusion
  230.7 6.1 %all-to-all-start.2 = ((bf16[64,2,128]{2,1,0:T(2,128)(2,1)}), bf16[64,2,128]{2,1,0:T(2,128)(2,1)S(1)}, u32[]{:S(2)}, u32[]{:S(2)}) async-start(bf16[64,2,128]{2,1,0:T(2,128)(2,1)} %bitcast.11), calls=%async_computation.3 | async-start | bytes 65536 | tf_op jit(solution)/shard_map/all_to_all | solution.py:73
  236.9 0.8 fusion.1
  237.7 0.8 fusion.2
  238.5 13.0 %all-to-all-done.2 = bf16[64,2,128]{2,1,0:T(2,128)(2,1)S(1)} async-done(((bf16[64,2,128]{2,1,0:T(2,128)(2,1)}), bf16[64,2,128]{2,1,0:T(2,128)(2,1)S(1)}, u32[]{:S(2)}, u32[]{:S(2)}) %all-to-all-start.2) | async-done | bytes 32800 | tf_op jit(solution)/shard_map/all_to_all | solution.py:73
  251.5 4.6 %all-to-all-start.5 = ((bf16[64,2,128]{2,1,0:T(2,128)(2,1)}), bf16[64,2,128]{2,1,0:T(2,128)(2,1)S(1)}, u32[]{:S(2)}, u32[]{:S(2)}) async-start(bf16[64,2,128]{2,1,0:T(2,128)(2,1)} %bitcast.24), calls=%async_computation.6 | async-start | bytes 65536 | tf_op jit(solution)/shard_map/all_to_all | solution.py:73
  256.2 14.7 %all-to-all-done.5 = bf16[64,2,128]{2,1,0:T(2,128)(2,1)S(1)} async-done(((bf16[64,2,128]{2,1,0:T(2,128)(2,1)}), bf16[64,2,128]{2,1,0:T(2,128)(2,1)S(1)}, u32[]{:S(2)}, u32[]{:S(2)}) %all-to-all-start.5) | async-done | bytes 32800 | tf_op jit(solution)/shard_map/all_to_all | solution.py:73
  270.9 4.6 %all-to-all-start.8 = ((bf16[64,2,128]{2,1,0:T(2,128)(2,1)}), bf16[64,2,128]{2,1,0:T(2,128)(2,1)S(1)}, u32[]{:S(2)}, u32[]{:S(2)}) async-start(bf16[64,2,128]{2,1,0:T(2,128)(2,1)} %bitcast.37), calls=%async_computation.9 | async-start | bytes 65536 | tf_op jit(solution)/shard_map/all_to_all | solution.py:73
  275.5 0.8 fusion.3
  276.3 0.9 fusion.11
  277.2 12.8 %all-to-all-done.8 = bf16[64,2,128]{2,1,0:T(2,128)(2,1)S(1)} async-done(((bf16[64,2,128]{2,1,0:T(2,128)(2,1)}), bf16[64,2,128]{2,1,0:T(2,128)(2,1)S(1)}, u32[]{:S(2)}, u32[]{:S(2)}) %all-to-all-start.8) | async-done | bytes 32800 | tf_op jit(solution)/shard_map/all_to_all | solution.py:73
  290.1 4.6 %all-to-all-start.11 = ((bf16[64,2,128]{2,1,0:T(2,128)(2,1)}), bf16[64,2,128]{2,1,0:T(2,128)(2,1)S(1)}, u32[]{:S(2)}, u32[]{:S(2)}) async-start(bf16[64,2,128]{2,1,0:T(2,128)(2,1)} %bitcast.50), calls=%async_computation.12 | async-start | bytes 65536 | tf_op jit(solution)/shard_map/all_to_all | solution.py:73
  294.7 0.9 fusion.10
  295.6 0.9 fusion.9
  296.6 12.8 %all-to-all-done.11 = bf16[64,2,128]{2,1,0:T(2,128)(2,1)S(1)} async-done(((bf16[64,2,128]{2,1,0:T(2,128)(2,1)}), bf16[64,2,128]{2,1,0:T(2,128)(2,1)S(1)}, u32[]{:S(2)}, u32[]{:S(2)}) %all-to-all-start.11) | async-done | bytes 32800 | tf_op jit(solution)/shard_map/all_to_all | solution.py:73
  309.3 0.9 fusion.8
  (101 shorter events, 7.6 us)
Async XLA Ops:
  6.5 209.1 %copy-start = (bf16[1024,1024]{1,0:T(8,128)(2,1)S(1)}, bf16[1024,1024]{1,0:T(8,128)(2,1)}, u32[]{:S(2)}) copy-start(bf16[1024,1024]{1,0:T(8,128)(2,1)} %param.7) | copy-start | bytes 6291460
  6.5 99.9 %copy-start.2 = (bf16[4,48,1024]{2,1,0:T(8,128)(2,1)S(1)}, bf16[4,48,1024]{2,1,0:T(8,128)(2,1)}, u32[]{:S(2)}) copy-start(bf16[4,48,1024]{2,1,0:T(8,128)(2,1)} %param.5) | copy-start | bytes 1179652
  9.3 97.4 %copy-start.12 = (s32[48]{0:T(128)}, s32[48]{0:T(128)S(1)}, u32[]{:S(2)}) copy-start(s32[48]{0:T(128)S(1)} %get-tuple-element.15) | copy-start | bytes 580
  9.3 97.4 %copy-start.14 = (s32[48]{0:T(128)}, s32[48]{0:T(128)S(1)}, u32[]{:S(2)}) copy-start(s32[48]{0:T(128)S(1)} %get-tuple-element.13) | copy-start | bytes 580
  9.3 122.3 %copy-start.10 = (s32[48]{0:T(128)}, s32[48]{0:T(128)S(1)}, u32[]{:S(2)}) copy-start(s32[48]{0:T(128)S(1)} %get-tuple-element.14) | copy-start | bytes 580
  9.3 145.4 %copy-start.8 = (s32[48]{0:T(128)}, s32[48]{0:T(128)S(1)}, u32[]{:S(2)}) copy-start(s32[48]{0:T(128)S(1)} %get-tuple-element.16) | copy-start | bytes 580
  10.3 33.1 %all-to-all-start = ((bf16[64,1,2]{2,1,0:T(2,128)(2,1)}), bf16[64,1,2]{2,1,0:T(2,128)(2,1)S(1)}, u32[]{:S(2)}, u32[]{:S(2)}) async-start(bf16[64,1,2]{2,1,0:T(2,128)(2,1)} %all_to_all.64), calls=%async_computation.1 | async-start | bytes 65536 | tf_op jit(solution)/shard_map/all_to_all | solution.py:64
  43.4 38.5 %copy-start.4 = (bf16[64,1,2]{2,1,0:T(2,128)(2,1)}, bf16[64,1,2]{2,1,0:T(2,128)(2,1)S(1)}, u32[]{:S(2)}) copy-start(bf16[64,1,2]{2,1,0:T(2,128)(2,1)S(1)} %all-to-all-done) | copy-start | bytes 772
  43.4 19.4 %all-to-all-start.3 = ((bf16[64,1,2]{2,1,0:T(2,128)(2,1)}), bf16[64,1,2]{2,1,0:T(2,128)(2,1)S(1)}, u32[]{:S(2)}, u32[]{:S(2)}) async-start(bf16[64,1,2]{2,1,0:T(2,128)(2,1)} %all_to_all.65), calls=%async_computation.4 | async-start | bytes 65536 | tf_op jit(solution)/shard_map/all_to_all | solution.py:64
  62.7 19.2 %copy-start.5 = (bf16[64,1,2]{2,1,0:T(2,128)(2,1)}, bf16[64,1,2]{2,1,0:T(2,128)(2,1)S(1)}, u32[]{:S(2)}) copy-start(bf16[64,1,2]{2,1,0:T(2,128)(2,1)S(1)} %all-to-all-done.3) | copy-start | bytes 772
  62.8 19.2 %all-to-all-start.6 = ((bf16[64,1,2]{2,1,0:T(2,128)(2,1)}), bf16[64,1,2]{2,1,0:T(2,128)(2,1)S(1)}, u32[]{:S(2)}, u32[]{:S(2)}) async-start(bf16[64,1,2]{2,1,0:T(2,128)(2,1)} %all_to_all.66), calls=%async_computation.7 | async-start | bytes 65536 | tf_op jit(solution)/shard_map/all_to_all | solution.py:64
  81.9 0.6 copy-start.6
  82.5 19.3 %all-to-all-start.9 = ((bf16[64,1,2]{2,1,0:T(2,128)(2,1)}), bf16[64,1,2]{2,1,0:T(2,128)(2,1)S(1)}, u32[]{:S(2)}, u32[]{:S(2)}) async-start(bf16[64,1,2]{2,1,0:T(2,128)(2,1)} %all_to_all.67), calls=%async_computation.10 | async-start | bytes 65536 | tf_op jit(solution)/shard_map/all_to_all | solution.py:64
  101.8 4.9 %copy-start.7 = (bf16[64,1,2]{2,1,0:T(2,128)(2,1)}, bf16[64,1,2]{2,1,0:T(2,128)(2,1)S(1)}, u32[]{:S(2)}) copy-start(bf16[64,1,2]{2,1,0:T(2,128)(2,1)S(1)} %all-to-all-done.9) | copy-start | bytes 772
  101.8 23.3 %all-to-all-start.1 = ((bf16[64,2,1024]{2,1,0:T(2,128)(2,1)}), bf16[64,2,1024]{2,1,0:T(2,128)(2,1)S(1)}, u32[]{:S(2)}, u32[]{:S(2)}) async-start(bf16[64,2,1024]{2,1,0:T(2,128)(2,1)} %reshape.453), calls=%async_computation.2 | async-start | bytes 524288 | tf_op jit(solution)/shard_map/all_to_all | solution.py:63
  107.5 71.4 %copy-start.1 = (bf16[4,1024,64]{1,2,0:T(8,128)(2,1)S(1)}, bf16[4,1024,64]{1,2,0:T(8,128)(2,1)}, u32[]{:S(2)}) copy-start(bf16[4,1024,64]{1,2,0:T(8,128)(2,1)} %param.8) | copy-start | bytes 1572868
  125.2 0.7 copy-start.3
  125.9 23.4 %all-to-all-start.4 = ((bf16[64,2,1024]{2,1,0:T(2,128)(2,1)}), bf16[64,2,1024]{2,1,0:T(2,128)(2,1)S(1)}, u32[]{:S(2)}, u32[]{:S(2)}) async-start(bf16[64,2,1024]{2,1,0:T(2,128)(2,1)} %reshape.457), calls=%async_computation.5 | async-start | bytes 524288 | tf_op jit(solution)/shard_map/all_to_all | solution.py:63
  149.3 24.1 %all-to-all-start.7 = ((bf16[64,2,1024]{2,1,0:T(2,128)(2,1)}), bf16[64,2,1024]{2,1,0:T(2,128)(2,1)}, u32[]{:S(2)}, u32[]{:S(2)}) async-start(bf16[64,2,1024]{2,1,0:T(2,128)(2,1)} %reshape.461), calls=%async_computation.8 | async-start | bytes 524288 | tf_op jit(solution)/shard_map/all_to_all | solution.py:63
  173.4 24.1 %all-to-all-start.10 = ((bf16[64,2,1024]{2,1,0:T(2,128)(2,1)}), bf16[64,2,1024]{2,1,0:T(2,128)(2,1)}, u32[]{:S(2)}, u32[]{:S(2)}) async-start(bf16[64,2,1024]{2,1,0:T(2,128)(2,1)} %reshape.465), calls=%async_computation.11 | async-start | bytes 524288 | tf_op jit(solution)/shard_map/all_to_all | solution.py:63
  178.8 97.5 %reduce-scatter.2.cloned.1.call-start = ((), (), s32[]{:S(2)}) async-start(), calls=%async_computation.13 | async-start | bytes 884736 | tf_op jit(solution)/shard_map/reduce_scatter | solution.py:36
  179.8 21.0 %collective-permute-start = (f32[128,64]{0,1:T(8,128)}, f32[128,64]{0,1:T(8,128)}, u32[]{:S(2)}, u32[]{:S(2)}) collective-permute-start(f32[128,64]{0,1:T(8,128)} %multiply_reduce_fusion.3), channel_id=1, source_target_pairs={{0,1},{1,0},{2,3},{3,2},{4,5},{5,4},{6,7},{7,6},{8,9},{9,8},{10,11... | collective-permute-start | bytes 98312 | tf_op jit(solution)/shard_map/ppermute | solution.py:18
  182.2 22.6 %collective-permute-start.3 = (f32[128,64]{0,1:T(8,128)S(1)}, f32[128,64]{0,1:T(8,128)S(1)}, u32[]{:S(2)}, u32[]{:S(2)}) collective-permute-start(f32[128,64]{0,1:T(8,128)S(1)} %multiply_reduce_fusion.2), channel_id=1, source_target_pairs={{0,1},{1,0},{2,3},{3,2},{4,5},{5,4},{6,7},{7,6},{8,9},{9,8},{10,11... | collective-permute-start | bytes 98312 | tf_op jit(solution)/shard_map/ppermute | solution.py:18
  186.0 21.5 %collective-permute-start.6 = (f32[128,64]{0,1:T(8,128)S(1)}, f32[128,64]{0,1:T(8,128)S(1)}, u32[]{:S(2)}, u32[]{:S(2)}) collective-permute-start(f32[128,64]{0,1:T(8,128)S(1)} %multiply_reduce_fusion.1), channel_id=1, source_target_pairs={{0,1},{1,0},{2,3},{3,2},{4,5},{5,4},{6,7},{7,6},{8,9},{9,8},{10,11... | collective-permute-start | bytes 98312 | tf_op jit(solution)/shard_map/ppermute | solution.py:18
  198.9 11.8 %collective-permute-start.9 = (f32[128,64]{0,1:T(8,128)S(1)}, f32[128,64]{0,1:T(8,128)S(1)}, u32[]{:S(2)}, u32[]{:S(2)}) collective-permute-start(f32[128,64]{0,1:T(8,128)S(1)} %multiply_reduce_fusion), channel_id=1, source_target_pairs={{0,1},{1,0},{2,3},{3,2},{4,5},{5,4},{6,7},{7,6},{8,9},{9,8},{10,11... | collective-permute-start | bytes 98312 | tf_op jit(solution)/shard_map/ppermute | solution.py:18
  201.6 11.8 %collective-permute-start.1 = (f32[128,64]{0,1:T(8,128)S(1)}, f32[128,64]{0,1:T(8,128)S(1)}, u32[]{:S(2)}, u32[]{:S(2)}) collective-permute-start(f32[128,64]{0,1:T(8,128)S(1)} %add.140), channel_id=1, source_target_pairs={{0,2},{1,3},{2,0},{3,1},{4,6},{5,7},{6,4},{7,5},{8,10},{9,11},{10,... | collective-permute-start | bytes 98312 | tf_op jit(solution)/shard_map/ppermute | solution.py:18
  204.8 12.5 %collective-permute-start.4 = (f32[128,64]{0,1:T(8,128)S(1)}, f32[128,64]{0,1:T(8,128)S(1)}, u32[]{:S(2)}, u32[]{:S(2)}) collective-permute-start(f32[128,64]{0,1:T(8,128)S(1)} %add.147), channel_id=1, source_target_pairs={{0,2},{1,3},{2,0},{3,1},{4,6},{5,7},{6,4},{7,5},{8,10},{9,11},{10,... | collective-permute-start | bytes 98312 | tf_op jit(solution)/shard_map/ppermute | solution.py:18
  207.5 14.9 %collective-permute-start.7 = (f32[128,64]{0,1:T(8,128)S(1)}, f32[128,64]{0,1:T(8,128)S(1)}, u32[]{:S(2)}, u32[]{:S(2)}) collective-permute-start(f32[128,64]{0,1:T(8,128)S(1)} %add.154), channel_id=1, source_target_pairs={{0,2},{1,3},{2,0},{3,1},{4,6},{5,7},{6,4},{7,5},{8,10},{9,11},{10,... | collective-permute-start | bytes 98312 | tf_op jit(solution)/shard_map/ppermute | solution.py:18
  210.7 14.0 %collective-permute-start.10 = (f32[128,64]{0,1:T(8,128)S(1)}, f32[128,64]{0,1:T(8,128)S(1)}, u32[]{:S(2)}, u32[]{:S(2)}) collective-permute-start(f32[128,64]{0,1:T(8,128)S(1)} %add.161), channel_id=1, source_target_pairs={{0,2},{1,3},{2,0},{3,1},{4,6},{5,7},{6,4},{7,5},{8,10},{9,11},{10,... | collective-permute-start | bytes 98312 | tf_op jit(solution)/shard_map/ppermute | solution.py:18
  213.4 16.4 %collective-permute-start.2 = (f32[128,64]{0,1:T(8,128)S(1)}, f32[128,64]{0,1:T(8,128)S(1)}, u32[]{:S(2)}, u32[]{:S(2)}) collective-permute-start(f32[128,64]{0,1:T(8,128)S(1)} %add.141), channel_id=1, source_target_pairs={{0,4},{1,5},{2,6},{3,7},{4,0},{5,1},{6,2},{7,3},{8,12},{9,13},{10,... | collective-permute-start | bytes 98312 | tf_op jit(solution)/shard_map/ppermute | solution.py:18
  215.6 14.2 %copy-start.19 = (bf16[128,4]{0,1:T(4,128)(2,1)S(1)}, bf16[128,4]{0,1:T(4,128)(2,1)}, u32[]{:S(2)}) copy-start(bf16[128,4]{0,1:T(4,128)(2,1)} %get-tuple-element.23) | copy-start | bytes 3076
  215.7 14.2 %copy-start.20 = (bf16[4,64,128]{2,1,0:T(8,128)(2,1)S(1)}, bf16[4,64,128]{2,1,0:T(8,128)(2,1)}, u32[]{:S(2)}) copy-start(bf16[4,64,128]{2,1,0:T(8,128)(2,1)} %param.9) | copy-start | bytes 196612
  215.7 21.2 %copy-start.18 = (bf16[128,4]{0,1:T(4,128)(2,1)S(1)}, bf16[128,4]{0,1:T(4,128)(2,1)}, u32[]{:S(2)}) copy-start(bf16[128,4]{0,1:T(4,128)(2,1)} %get-tuple-element.32) | copy-start | bytes 3076
  215.7 22.0 %copy-start.17 = (bf16[128,4]{0,1:T(4,128)(2,1)S(1)}, bf16[128,4]{0,1:T(4,128)(2,1)}, u32[]{:S(2)}) copy-start(bf16[128,4]{0,1:T(4,128)(2,1)} %get-tuple-element.34) | copy-start | bytes 3076
  215.7 59.8 %copy-start.16 = (bf16[128,4]{0,1:T(4,128)(2,1)S(1)}, bf16[128,4]{0,1:T(4,128)(2,1)}, u32[]{:S(2)}) copy-start(bf16[128,4]{0,1:T(4,128)(2,1)} %get-tuple-element.36) | copy-start | bytes 3076
  215.7 60.6 %copy-start.15 = (s32[48]{0:T(128)S(1)}, s32[48]{0:T(128)}, u32[]{:S(2)}) copy-start(s32[48]{0:T(128)} %copy-done.14) | copy-start | bytes 580
  215.7 79.0 %copy-start.13 = (s32[48]{0:T(128)S(1)}, s32[48]{0:T(128)}, u32[]{:S(2)}) copy-start(s32[48]{0:T(128)} %copy-done.12) | copy-start | bytes 580
  215.7 79.9 %copy-start.11 = (s32[48]{0:T(128)S(1)}, s32[48]{0:T(128)}, u32[]{:S(2)}) copy-start(s32[48]{0:T(128)} %copy-done.10) | copy-start | bytes 580
  215.7 93.6 %copy-start.9 = (s32[48]{0:T(128)S(1)}, s32[48]{0:T(128)}, u32[]{:S(2)}) copy-start(s32[48]{0:T(128)} %copy-done.8) | copy-start | bytes 580
  217.3 19.5 %collective-permute-start.5 = (f32[128,64]{0,1:T(8,128)S(1)}, f32[128,64]{0,1:T(8,128)S(1)}, u32[]{:S(2)}, u32[]{:S(2)}) collective-permute-start(f32[128,64]{0,1:T(8,128)S(1)} %add.148), channel_id=1, source_target_pairs={{0,4},{1,5},{2,6},{3,7},{4,0},{5,1},{6,2},{7,3},{8,12},{9,13},{10,... | collective-permute-start | bytes 98312 | tf_op jit(solution)/shard_map/ppermute | solution.py:18
  222.4 14.4 %collective-permute-start.8 = (f32[128,64]{0,1:T(8,128)S(1)}, f32[128,64]{0,1:T(8,128)S(1)}, u32[]{:S(2)}, u32[]{:S(2)}) collective-permute-start(f32[128,64]{0,1:T(8,128)S(1)} %add.155), channel_id=1, source_target_pairs={{0,4},{1,5},{2,6},{3,7},{4,0},{5,1},{6,2},{7,3},{8,12},{9,13},{10,... | collective-permute-start | bytes 98312 | tf_op jit(solution)/shard_map/ppermute | solution.py:18
  224.7 31.4 %collective-permute-start.11 = (f32[128,64]{0,1:T(8,128)S(1)}, f32[128,64]{0,1:T(8,128)S(1)}, u32[]{:S(2)}, u32[]{:S(2)}) collective-permute-start(f32[128,64]{0,1:T(8,128)S(1)} %add.162), channel_id=1, source_target_pairs={{0,4},{1,5},{2,6},{3,7},{4,0},{5,1},{6,2},{7,3},{8,12},{9,13},{10,... | collective-permute-start | bytes 98312 | tf_op jit(solution)/shard_map/ppermute | solution.py:18
  230.7 20.9 %all-to-all-start.2 = ((bf16[64,2,128]{2,1,0:T(2,128)(2,1)}), bf16[64,2,128]{2,1,0:T(2,128)(2,1)S(1)}, u32[]{:S(2)}, u32[]{:S(2)}) async-start(bf16[64,2,128]{2,1,0:T(2,128)(2,1)} %bitcast.11), calls=%async_computation.3 | async-start | bytes 65536 | tf_op jit(solution)/shard_map/all_to_all | solution.py:73
  251.5 19.3 %all-to-all-start.5 = ((bf16[64,2,128]{2,1,0:T(2,128)(2,1)}), bf16[64,2,128]{2,1,0:T(2,128)(2,1)S(1)}, u32[]{:S(2)}, u32[]{:S(2)}) async-start(bf16[64,2,128]{2,1,0:T(2,128)(2,1)} %bitcast.24), calls=%async_computation.6 | async-start | bytes 65536 | tf_op jit(solution)/shard_map/all_to_all | solution.py:73
  270.9 19.2 %all-to-all-start.8 = ((bf16[64,2,128]{2,1,0:T(2,128)(2,1)}), bf16[64,2,128]{2,1,0:T(2,128)(2,1)S(1)}, u32[]{:S(2)}, u32[]{:S(2)}) async-start(bf16[64,2,128]{2,1,0:T(2,128)(2,1)} %bitcast.37), calls=%async_computation.9 | async-start | bytes 65536 | tf_op jit(solution)/shard_map/all_to_all | solution.py:73
  290.1 19.3 %all-to-all-start.11 = ((bf16[64,2,128]{2,1,0:T(2,128)(2,1)}), bf16[64,2,128]{2,1,0:T(2,128)(2,1)S(1)}, u32[]{:S(2)}, u32[]{:S(2)}) async-start(bf16[64,2,128]{2,1,0:T(2,128)(2,1)} %bitcast.50), calls=%async_computation.12 | async-start | bytes 65536 | tf_op jit(solution)/shard_map/all_to_all | solution.py:73
Sparse Core Ops, SparseCore 0:
  217.4 27.3 reduce-scatter.1
